TPU v7x, 128 devices: a whole 4x4x4 slice. The times are simulated.
128 devices in a mesh: gx: 8 (over y, core), gy: 16 (over z, x).
Axes of the slice: x: 4, y: 4, z: 4, core: 2. Of those that a mesh axis runs over, the one named last changes fastest.
Arguments:
- stored: bfloat16 [128, 4096, 360], P(('gx', 'gy')), may hold values from -6 to 6
- counts: int32 [128, 128], P(('gx', 'gy')), may hold values from 0 to 32, as said below
- owners: int32 [128, 2048], P('gx', 'gy'), may hold values from 0 to 4095, as said below
- land_mask: int32 [128, 2048], P('gx', 'gy'), may hold values 0 or 1
- flow_x: float32 [128, 2048], P('gx', 'gy'), may hold values from -4 to 4
- flow_y: float32 [128, 2048], P('gx', 'gy'), may hold values from -4 to 4
- costate: float32 [3, 60, 128, 2048], P(None, None, 'gx', 'gy'), may hold values from -6 to 6
- weight_in: float32 [180, 256], replicated, may hold values from -0.4375 to 0.4375
- bias_in: float32 [256], replicated, may hold values from -3 to 3
- weight_mid: float32 [256, 256], replicated, may hold values from -0.375 to 0.375
- bias_mid: float32 [256], replicated, may hold values from -3 to 3
- weight_out: float32 [256, 60], replicated, may hold values from -0.375 to 0.375
- bias_out: float32 [60], replicated, may hold values from -4 to 4
Outputs:
- adjoint: float32 [3, 60, 128, 2048], P(None, None, 'gx', 'gy')
- grad_weight_in: float32 [180, 256], replicated
- grad_bias_in: float32 [256], replicated
- grad_weight_mid: float32 [256, 256], replicated
- grad_bias_mid: float32 [256], replicated
- grad_weight_out: float32 [256, 60], replicated
- grad_bias_out: float32 [60], replicated
Inputs may be any that keep to these rules, and one draw needn't show every extreme that they name: counts[s, d] rows of device s belong to tile d; over s they sum to 2048 for every tile; some tile takes exactly 32 rows from one device. owners[x, y] = s * 32 + r with r < counts[s, d] for the column's tile d; within a tile every value appears once.
All inputs are finite; a program needn't handle non-finite values. No bound on the sum of `land_mask` on one device may be relied on, other than what follows from the above.
Results may differ from a plain program's by a relative error of at most 0.0003.
Values may be sent and summed in bfloat16 or wider, within the bound.
No kernel may reach another device: no remote copies, remote signals or barrier semaphores. Data moves between devices by JAX's collectives and lax.ppermute only.
A program may use at most 128 MiB of HBM per device.

v0:
```python
import jax
import jax.numpy as jnp
from jax import lax
from jax.sharding import PartitionSpec as P

NZ = 60
TRACERS = 3
TSTEPS = 2
IN = 180
step_size = 0.25
flat_mix = 0.25
kappa_top = 1.5


def padded_2(value, sides, width):
    for axis, dim in sides:
        count, length = (lax.axis_size(axis), value.shape[dim])
        up = [(i, (i + 1) % count) for i in range(count - 1)]
        down = [(j, i) for i, j in up]
        last = lax.slice_in_dim(value, length - width, length, axis=dim)
        initial = lax.slice_in_dim(value, 0, width, axis=dim)
        before = lax.ppermute(last, axis, up)
        after = lax.ppermute(initial, axis, down)
        value = jnp.concatenate([before, value, after], axis=dim)
    return value


def vertical(columns, params):
    weight_in, bias_in, weight_mid, bias_mid, weight_out, bias_out = params
    hp = lax.Precision.HIGHEST
    first = jnp.tanh(jnp.dot(weight_in.T, columns, precision=hp) + bias_in[:, None])
    second = jnp.tanh(jnp.dot(weight_mid.T, first, precision=hp) + bias_mid[:, None])
    kappa = kappa_top * jax.nn.sigmoid(
        jnp.dot(weight_out.T, second, precision=hp) + bias_out[:, None]
    )
    field = columns.reshape(TRACERS, NZ, columns.shape[1])
    flux = kappa[None, :-1, :] * (field[:, 1:, :] - field[:, :-1, :])
    edge = jnp.zeros_like(flux[:, :1, :])
    upper = jnp.concatenate([flux, edge], axis=1)
    lower = jnp.concatenate([edge, flux], axis=1)
    return (upper - lower).reshape(columns.shape)


def transport(padded, padded_x, padded_y, weighted):
    near = (
        padded[..., 2:, 1:-1]
        + padded[..., :-2, 1:-1]
        + padded[..., 1:-1, 2:]
        + padded[..., 1:-1, :-2]
    )
    result = flat_mix * (near - 4.0 * weighted)
    result = result + 0.5 * (padded_x[..., 2:, 1:-1] - padded_x[..., :-2, 1:-1])
    return result + 0.5 * (padded_y[..., 1:-1, 2:] - padded_y[..., 1:-1, :-2])


def on_device(
    stored,
    counts,
    owners,
    land_mask,
    flow_x,
    flow_y,
    costate,
    weight_in,
    bias_in,
    weight_mid,
    bias_mid,
    weight_out,
    bias_out,
):
    width_x = lax.axis_size("gx")
    width_y = lax.axis_size("gy")
    devices = width_x * width_y
    tile_x, tile_y = owners.shape
    ncols = tile_x * tile_y
    slot = 2 * ncols // devices
    feat = stored.shape[2]
    my_counts = counts[0]
    starts = jnp.cumsum(my_counts) - my_counts
    row_index = jnp.minimum(
        starts[:, None] + jnp.arange(slot, dtype=jnp.int32)[None, :], stored.shape[1] - 1
    )
    outgoing = stored[0][row_index]
    arrived = lax.all_to_all(outgoing, ("gx", "gy"), split_axis=0, concat_axis=0, tiled=True)
    picked = arrived.reshape(devices * slot, feat)[owners.reshape(-1)]
    states = picked.T.reshape(TSTEPS, TRACERS, NZ, tile_x, tile_y).astype(jnp.float32)
    params = (weight_in, bias_in, weight_mid, bias_mid, weight_out, bias_out)
    totals = jax.tree.map(jnp.zeros_like, params)
    ocean = land_mask.astype(jnp.float32)
    lam = costate
    for moment in range(TSTEPS - 1, -1, -1):
        state = states[moment]
        weighted = lam * ocean
        stacked = jnp.stack([weighted, flow_x * weighted, flow_y * weighted])
        padded = padded_2(stacked, (("gx", 3), ("gy", 4)), 1)
        across = transport(padded[0], padded[1], padded[2], weighted)
        unused, pullback = jax.vjp(vertical, state.reshape(IN, ncols), params)
        grad_state, grad_params = pullback(weighted.reshape(IN, ncols))
        down = grad_state.reshape(TRACERS, NZ, tile_x, tile_y)
        lam = lam + step_size * (across + down)
        totals = jax.tree.map(lambda left, right: left + step_size * right, totals, grad_params)
    summed = lax.psum(
        (totals[0], totals[1], totals[2], totals[3], totals[4], totals[5]), ("gx", "gy")
    )
    scale = 1.0 / jnp.sqrt(jnp.float32(ncols * devices))
    return (
        lam,
        summed[0] * scale,
        summed[1] * scale,
        summed[2] * scale,
        summed[3] * scale,
        summed[4] * scale,
        summed[5] * scale,
    )


def solution(mesh):
    in_specs = (
        P(("gx", "gy"), None, None),
        P(("gx", "gy"), None),
        P("gx", "gy"),
        P("gx", "gy"),
        P("gx", "gy"),
        P("gx", "gy"),
        P(None, None, "gx", "gy"),
        P(),
        P(),
        P(),
        P(),
        P(),
        P(),
    )
    out_specs = (P(None, None, "gx", "gy"), P(), P(), P(), P(), P(), P())
    return jax.shard_map(
        on_device, mesh=mesh, in_specs=in_specs, out_specs=out_specs, check_vma=False
    )
```

profile of v0, /device:TPU:32, one launch (start us, length us, event | category | flops | bytes accessed | tf_op | source)
XLA Modules:
  0.0 549.9 jit_solution(17194821409840462331)
XLA Ops:
  7.9 2.9 fusion.48
  13.1 2.4 collective-permute-start
  17.0 3.4 copy.68
  21.0 17.1 %gather_fusion = bf16[4096,360]{1,0:T(8,128)(2,1)} fusion(bf16[4096,360]{1,0:T(8,128)(2,1)S(1)} %bitcast.88, s32[4096]{0:T(1024)S(1)} %broadcast_clamp_fusion), kind=kCustom, calls=%fused_computation | custom fusion | bytes 5914624 | tf_op jit(solution)/shard_map/gather | solution.py:83
  38.1 11.9 %all-to-all-start = ((bf16[128,32,360]{2,1,0:T(8,128)(2,1)}), bf16[128,32,360]{2,1,0:T(8,128)(2,1)S(1)}, u32[]{:S(2)}, u32[]{:S(2)}) async-start(bf16[128,32,360]{2,1,0:T(8,128)(2,1)} %bitcast.94), calls=%async_computation | async-start | bytes 6291456 | tf_op jit(solution)/shard_map/all_to_all | solution.py:84
  50.1 5.1 pad_maximum_fusion.2
  55.2 11.3 %fusion.61 = (f32[3,3,60,18,1]{4,3,2,1,0:T(8,128)}, f32[3,3,60,18,1]{4,3,2,1,0:T(8,128)}) fusion(f32[3,3,60,18,128]{4,3,2,1,0:T(8,128)} %pad_maximum_fusion.2), kind=kLoop, calls=%fused_computation.134 | loop fusion | bytes 155520 | tf_op jit(solution)/shard_map/slice | solution.py:20
  66.6 4.5 copy.64
  71.1 3.4 collective-permute-start.2
  74.5 5.2 copy.65
  79.7 4.8 collective-permute-start.3
  84.4 2.7 reshape_reshape.6
  89.1 5.2 copy.66
  94.3 5.3 copy.67
  99.6 16.7 %pad_maximum_fusion = f32[3,3,60,18,130]{4,3,2,1,0:T(8,128)} fusion(f32[3,3,60,18,1]{4,3,2,1,0:T(8,128)} %copy.67, f32[3,3,60,1,128]{4,3,2,1,0:T(1,128)} %collective-permute-done.1, f32[1,3,60,16,128]{4,3,2,1,0:T(8,128)} %copy-done.14, f32[1,3,60,16,128]{4,3,2,1,0:T(8,128)} %copy-done.13, f32[1,3,60,16,128]{4,3,2,1,0:T(8,128)} %copy-done.12, ...), kind=kLoop, calls=%fused_computation.2 | loop fusion | flops 7581600 | bytes 10108800 | tf_op jit(solution)/shard_map/concatenate | solution.py:24
  116.2 9.9 %slice_bitcast_fusion.5 = (f32[3,60,18,130]{3,2,1,0:T(8,128)}, f32[3,60,18,130]{3,2,1,0:T(8,128)}, f32[3,60,18,130]{3,2,1,0:T(8,128)}) fusion(f32[3,3,60,18,130]{4,3,2,1,0:T(8,128)} %pad_maximum_fusion), kind=kLoop, calls=%fused_computation.11 | loop fusion | bytes 10108800 | tf_op jit(solution)/shard_map/squeeze | solution.py:96
  126.1 9.3 %gather_fusion.1 = bf16[2048,360]{1,0:T(8,128)(2,1)} fusion(bf16[4096,360]{1,0:T(8,128)(2,1)S(1)} %bitcast.89, s32[2048]{0:T(1024)S(1)} %broadcast_clamp_fusion.1), kind=kCustom, calls=%fused_computation.1 | custom fusion | bytes 2957312 | tf_op jit(solution)/shard_map/gather | solution.py:85
  146.6 2.7 fusion.62
  149.3 3.2 copy.70
  152.6 2.8 reshape_reshape_squeeze.6
  155.4 2.9 fusion.59
  162.7 3.9 fusion.63
  168.2 4.5 fusion.4
  174.3 11.8 %fusion.49 = (f32[1,3,60,16,128]{4,3,2,1,0:T(8,128)}, f32[3,60,16,128]{3,2,1,0:T(8,128)S(1)}) fusion(f32[16,128]{1,0:T(8,128)S(1)} %convert_element_type.7, f32[3,60,16,128]{3,2,1,0:T(8,128)S(1)} %copy-done.30, f32[3,60,16,128]{3,2,1,0:T(8,128)S(1)} %bitcast.100, f32[3,60,18,130]{3,2,1,0:T(8,128)} %get-tuple-element.37, ...), kind=kLoop, calls=%fused_computation.106 | loop fusion | flops 6266880 | bytes 17702912 | tf_op jit(solution)/shard_map/stack | solution.py:94
  188.2 2.7 reshape_reshape.7
  190.9 3.5 fusion
  199.7 2.9 copy.75
  202.6 2.7 reshape_reshape_squeeze.7
  205.3 5.9 %fusion.58 = (f32[3,59,2048]{2,1,0:T(8,128)}, f32[3,59,2048]{2,1,0:T(8,128)}, f32[59,2048]{1,0:T(8,128)S(1)}) fusion(f32[3,60,2048]{2,1,0:T(8,128)} %reshape_reshape.7, f32[59,2048]{1,0:T(8,128)} %slice_multiply_fusion, f32[3,60,2048]{2,1,0:T(8,128)} %reshape_reshape_squeeze.7), kind=kLoop, calls=%fused_computation.131 | loop fusion | flops 2416640 | bytes 9666560 | tf_op jit(solution)/shard_map/transpose(jvp())/neg | solution.py:37
  213.6 4.3 fusion.67
  221.9 3.3 fusion.64
  225.3 65.3 %all-reduce.6 = (f32[256]{0:T(256)S(1)}, f32[256]{0:T(256)S(1)}, f32[256,60]{0,1:T(8,128)S(1)}, f32[60]{0:T(128)S(1)}) all-reduce(f32[256]{0:T(256)S(1)} %add_multiply_fusion.1, f32[256]{0:T(256)S(1)} %add_multiply_fusion, f32[256,60]{0,1:T(8,128)S(1)} %fusion.40, ...), channel_id=1, replica_groups=mesh['gx'=8,'gy'=16] {'gx','gy'}, use_global_device_ids=true, to_apply=%region_6.7 | all-reduce | flops 15932 | bytes 127456 | tf_op jit(solution)/shard_map/psum | solution.py:102
  291.2 6.5 %fusion.38 = f32[256,256]{1,0:T(8,128)} fusion(f32[256,256]{1,0:T(8,128)} %fusion.67, f32[2048,256]{1,0:T(8,128)} %fusion.2, f32[2048,256]{1,0:T(8,128)} %copy-done.19), kind=kOutput, calls=%fused_computation.85 | convolution fusion | flops 1610743808 | bytes 4718592 | tf_op jit(solution)/shard_map/transpose(jvp())/dot_general | solution.py:32
  304.0 2.7 reshape.182
  306.6 3.7 fusion.39
  310.3 4.3 fusion.5
  317.3 140.6 %all-reduce.10.cloned.1.call-done = (f32[180,256]{1,0:T(8,128)}, f32[256,256]{1,0:T(8,128)}) async-done(((f32[180,256]{1,0:T(8,128)}, f32[256,256]{1,0:T(8,128)}), (f32[180,256]{1,0:T(8,128)}, f32[256,256]{1,0:T(8,128)})) %all-reduce.10.cloned.1.call-update) | async-done | bytes 446480 | tf_op jit(solution)/shard_map/psum | solution.py:102
  459.6 4.9 pad_maximum_fusion.3
  464.5 11.3 %fusion.60 = (f32[3,3,60,18,1]{4,3,2,1,0:T(8,128)}, f32[3,3,60,18,1]{4,3,2,1,0:T(8,128)}) fusion(f32[3,3,60,18,128]{4,3,2,1,0:T(8,128)} %pad_maximum_fusion.3), kind=kLoop, calls=%fused_computation.133 | loop fusion | bytes 155520 | tf_op jit(solution)/shard_map/slice | solution.py:20
  475.8 4.5 copy.71
  480.4 3.2 collective-permute-start.6
  483.5 5.2 copy.72
  488.8 4.8 collective-permute-start.7
  494.3 5.2 copy.73
  499.4 5.3 copy.74
  504.7 16.2 %pad_maximum_fusion.1 = f32[3,3,60,18,130]{4,3,2,1,0:T(8,128)} fusion(f32[3,3,60,18,1]{4,3,2,1,0:T(8,128)} %copy.74, f32[3,3,60,1,128]{4,3,2,1,0:T(1,128)} %collective-permute-done.5, f32[1,3,60,16,128]{4,3,2,1,0:T(8,128)S(1)} %copy-done.11, f32[1,3,60,16,128]{4,3,2,1,0:T(8,128)S(1)} %get-tuple-element.51, f32[1,3,60,16,128]{4,3,2,1,0:T(8,128)} %get-tuple-element.27, ...), kind=kLoop, calls=%fused_computation.3 | loop fusion | flops 7581600 | bytes 10108800 | tf_op jit(solution)/shard_map/concatenate | solution.py:24
  520.8 10.1 %slice_bitcast_fusion.2 = (f32[3,60,18,130]{3,2,1,0:T(8,128)}, f32[3,60,18,130]{3,2,1,0:T(8,128)}, f32[3,60,18,130]{3,2,1,0:T(8,128)}) fusion(f32[3,3,60,18,130]{4,3,2,1,0:T(8,128)} %pad_maximum_fusion.1), kind=kLoop, calls=%fused_computation.8 | loop fusion | bytes 10108800 | tf_op jit(solution)/shard_map/squeeze | solution.py:96
  530.9 11.7 %fusion.24 = f32[3,60,16,128]{3,2,1,0:T(8,128)} fusion(f32[3,60,16,128]{3,2,1,0:T(8,128)S(1)} %copy-done.22, f32[3,60,16,128]{3,2,1,0:T(8,128)S(1)} %bitcast.99, f32[3,60,18,130]{3,2,1,0:T(8,128)} %get-tuple-element.34, f32[3,60,18,130]{3,2,1,0:T(8,128)} %get-tuple-element.35, f32[3,60,18,130]{3,2,1,0:T(8,128)} %get-tuple-element.33, ...), kind=kLoop, calls=%fused_computation.57 | loop fusion | flops 5898240 | bytes 16228352 | tf_op jit(solution)/shard_map/add | solution.py:100
  (147 shorter events, 51.3 us)
Async XLA Ops:
  7.2 133.6 %copy-start = (f32[256,256]{1,0:T(8,128)S(1)}, f32[256,256]{1,0:T(8,128)}, u32[]{:S(2)}) copy-start(f32[256,256]{1,0:T(8,128)} %param.22) | copy-start | bytes 786436
  10.8 2.2 copy-start.14
  13.1 37.0 %collective-permute-start = (f32[3,3,60,1,128]{4,3,2,1,0:T(1,128)}, f32[3,3,60,1,128]{4,3,2,1,0:T(1,128)}, u32[]{:S(2)}, u32[]{:S(2)}) collective-permute-start(f32[3,3,60,1,128]{4,3,2,1,0:T(1,128)} %get-tuple-element.45), channel_id=1, source_target_pairs={{0,16},{16,32},{32,48},{48,64},{64,80},{80,96},{96,112},{1,17},{17... | collective-permute-start | bytes 829448 | tf_op jit(solution)/shard_map/ppermute | solution.py:22
  15.5 4.8 copy-start.43
  15.5 34.6 %collective-permute-start.1 = (f32[3,3,60,1,128]{4,3,2,1,0:T(1,128)}, f32[3,3,60,1,128]{4,3,2,1,0:T(1,128)}, u32[]{:S(2)}, u32[]{:S(2)}) collective-permute-start(f32[3,3,60,1,128]{4,3,2,1,0:T(1,128)} %get-tuple-element.46), channel_id=1, source_target_pairs={{16,0},{32,16},{48,32},{64,48},{80,64},{96,80},{112,96},{17,1},{33... | collective-permute-start | bytes 829448 | tf_op jit(solution)/shard_map/ppermute | solution.py:23
  38.1 12.0 %copy-start.37 = (s32[16,128]{1,0:T(8,128)S(1)}, s32[16,128]{1,0:T(8,128)}, u32[]{:S(2)}) copy-start(s32[16,128]{1,0:T(8,128)} %param.15) | copy-start | bytes 24580
  38.1 88.0 %all-to-all-start = ((bf16[128,32,360]{2,1,0:T(8,128)(2,1)}), bf16[128,32,360]{2,1,0:T(8,128)(2,1)S(1)}, u32[]{:S(2)}, u32[]{:S(2)}) async-start(bf16[128,32,360]{2,1,0:T(8,128)(2,1)} %bitcast.94), calls=%async_computation | async-start | bytes 6291456 | tf_op jit(solution)/shard_map/all_to_all | solution.py:84
  50.0 407.9 %all-reduce.10.cloned.1.call-start = ((), (), s32[]{:S(2)}) async-start(), calls=%async_computation.1 | async-start | bytes 901120 | tf_op jit(solution)/shard_map/psum | solution.py:102
  71.1 18.0 %collective-permute-start.2 = (f32[3,3,60,18,1]{2,4,3,1,0:T(1,128)S(1)}, f32[3,3,60,18,1]{2,4,3,1,0:T(1,128)}, u32[]{:S(2)}, u32[]{:S(2)}) collective-permute-start(f32[3,3,60,18,1]{2,4,3,1,0:T(1,128)S(1)} %copy.64), channel_id=1, source_target_pairs={{0,1},{1,2},{2,3},{3,4},{4,5},{5,6},{6,7},{7,8},{8,9},{9,10},{10,1... | collective-permute-start | bytes 116648 | tf_op jit(solution)/shard_map/ppermute | solution.py:22
  79.7 14.6 %collective-permute-start.3 = (f32[3,3,60,18,1]{2,4,3,1,0:T(1,128)}, f32[3,3,60,18,1]{2,4,3,1,0:T(1,128)}, u32[]{:S(2)}, u32[]{:S(2)}) collective-permute-start(f32[3,3,60,18,1]{2,4,3,1,0:T(1,128)} %copy.65), channel_id=1, source_target_pairs={{1,0},{2,1},{3,2},{4,3},{5,4},{6,5},{7,6},{8,7},{9,8},{10,9},{11,1... | collective-permute-start | bytes 116648 | tf_op jit(solution)/shard_map/ppermute | solution.py:23
  135.4 1.9 copy-start.1
  135.5 1.9 copy-start.31
  135.5 1.9 copy-start.38
  138.4 4.3 copy-start.3
  138.4 2.4 copy-start.39
  140.8 1.9 copy-start.33
  140.8 1.9 copy-start.41
  142.7 2.2 copy-start.8
  152.6 2.8 copy-start.20
  155.4 2.9 copy-start.9
  155.4 2.9 copy-start.26
  160.4 2.1 copy-start.16
  160.4 2.3 copy-start.4
  174.3 11.8 %copy-start.35 = (f32[16,128]{1,0:T(8,128)S(1)}, f32[16,128]{1,0:T(8,128)}, u32[]{:S(2)}) copy-start(f32[16,128]{1,0:T(8,128)} %param.17) | copy-start | bytes 24580
  174.3 11.8 %copy-start.36 = (f32[16,128]{1,0:T(8,128)S(1)}, f32[16,128]{1,0:T(8,128)}, u32[]{:S(2)}) copy-start(f32[16,128]{1,0:T(8,128)} %param.18) | copy-start | bytes 24580
  186.1 2.1 copy-start.21
  190.9 4.9 copy-start.42
  205.3 5.9 %copy-start.24 = (f32[60,2048]{1,0:T(8,128)S(1)}, f32[60,2048]{1,0:T(8,128)}, u32[]{:S(2)}) copy-start(f32[60,2048]{1,0:T(8,128)} %copy-done.23) | copy-start | bytes 1474564
  205.3 6.1 %copy-start.7 = (f32[2048,256]{1,0:T(8,128)S(1)}, f32[2048,256]{1,0:T(8,128)}, u32[]{:S(2)}) copy-start(f32[2048,256]{1,0:T(8,128)} %copy-done.6) | copy-start | bytes 6291460
  211.4 2.1 copy-start.5
  211.4 2.2 copy-start.17
  213.6 8.1 %copy-start.19 = (f32[2048,256]{1,0:T(8,128)}, f32[2048,256]{1,0:T(8,128)S(1)}, u32[]{:S(2)}) copy-start(f32[2048,256]{1,0:T(8,128)S(1)} %get-tuple-element.65) | copy-start | bytes 6291460
  213.6 4.3 copy-start.18
  221.9 3.3 copy-start.44
  221.9 3.3 copy-start.40
  291.2 6.5 %copy-start.10 = (f32[1,3,60,16,128]{4,3,2,1,0:T(8,128)S(1)}, f32[1,3,60,16,128]{4,3,2,1,0:T(8,128)}, u32[]{:S(2)}) copy-start(f32[1,3,60,16,128]{4,3,2,1,0:T(8,128)} %get-tuple-element.52) | copy-start | bytes 4423684
  291.2 6.5 %copy-start.15 = (f32[1,3,60,16,128]{4,3,2,1,0:T(8,128)S(1)}, f32[1,3,60,16,128]{4,3,2,1,0:T(8,128)}, u32[]{:S(2)}) copy-start(f32[1,3,60,16,128]{4,3,2,1,0:T(8,128)} %get-tuple-element.27) | copy-start | bytes 4423684
  297.7 4.8 copy-start.27
  297.7 4.8 copy-start.28
  298.9 160.6 %collective-permute-start.4 = (f32[3,3,60,1,128]{4,3,2,1,0:T(1,128)}, f32[3,3,60,1,128]{4,3,2,1,0:T(1,128)}, u32[]{:S(2)}, u32[]{:S(2)}) collective-permute-start(f32[3,3,60,1,128]{4,3,2,1,0:T(1,128)} %get-tuple-element.43), channel_id=1, source_target_pairs={{0,16},{16,32},{32,48},{48,64},{64,80},{80,96},{96,112},{1,17},{17... | collective-permute-start | bytes 829448 | tf_op jit(solution)/shard_map/ppermute | solution.py:22
  301.2 158.3 %collective-permute-start.5 = (f32[3,3,60,1,128]{4,3,2,1,0:T(1,128)}, f32[3,3,60,1,128]{4,3,2,1,0:T(1,128)}, u32[]{:S(2)}, u32[]{:S(2)}) collective-permute-start(f32[3,3,60,1,128]{4,3,2,1,0:T(1,128)} %get-tuple-element.44), channel_id=1, source_target_pairs={{16,0},{32,16},{48,32},{64,48},{80,64},{96,80},{112,96},{17,1},{33... | collective-permute-start | bytes 829448 | tf_op jit(solution)/shard_map/ppermute | solution.py:23
  306.6 3.7 copy-start.32
  316.0 143.6 %copy-start.11 = (f32[1,3,60,16,128]{4,3,2,1,0:T(8,128)S(1)}, f32[1,3,60,16,128]{4,3,2,1,0:T(8,128)}, u32[]{:S(2)}) copy-start(f32[1,3,60,16,128]{4,3,2,1,0:T(8,128)} %get-tuple-element.52) | copy-start | bytes 4423684
  480.4 13.9 %collective-permute-start.6 = (f32[3,3,60,18,1]{2,4,3,1,0:T(1,128)S(1)}, f32[3,3,60,18,1]{2,4,3,1,0:T(1,128)}, u32[]{:S(2)}, u32[]{:S(2)}) collective-permute-start(f32[3,3,60,18,1]{2,4,3,1,0:T(1,128)S(1)} %copy.71), channel_id=1, source_target_pairs={{0,1},{1,2},{2,3},{3,4},{4,5},{5,6},{6,7},{7,8},{8,9},{9,10},{10,1... | collective-permute-start | bytes 116648 | tf_op jit(solution)/shard_map/ppermute | solution.py:22
  483.5 10.0 %copy-start.34 = (f32[180,256]{1,0:T(8,128)S(1)}, f32[180,256]{1,0:T(8,128)}, u32[]{:S(2)}) copy-start(f32[180,256]{1,0:T(8,128)} %get-tuple-element.25) | copy-start | bytes 552964
  488.8 10.7 %collective-permute-start.7 = (f32[3,3,60,18,1]{2,4,3,1,0:T(1,128)}, f32[3,3,60,18,1]{2,4,3,1,0:T(1,128)}, u32[]{:S(2)}, u32[]{:S(2)}) collective-permute-start(f32[3,3,60,18,1]{2,4,3,1,0:T(1,128)} %copy.72), channel_id=1, source_target_pairs={{1,0},{2,1},{3,2},{4,3},{5,4},{6,5},{7,6},{8,7},{9,8},{10,9},{11,1... | collective-permute-start | bytes 116648 | tf_op jit(solution)/shard_map/ppermute | solution.py:23
  520.8 10.1 %copy-start.22 = (f32[3,60,16,128]{3,2,1,0:T(8,128)S(1)}, f32[3,60,16,128]{3,2,1,0:T(8,128)}, u32[]{:S(2)}) copy-start(f32[3,60,16,128]{3,2,1,0:T(8,128)} %copy-done.21) | copy-start | bytes 4423684
  520.8 10.1 %copy-start.29 = (f32[180,16,128]{2,1,0:T(8,128)S(1)}, f32[180,16,128]{2,1,0:T(8,128)}, u32[]{:S(2)}) copy-start(f32[180,16,128]{2,1,0:T(8,128)} %slice.203) | copy-start | bytes 4423684
  (7 other events, 9.3 us)
Sparse Core Ops, SparseCore 0:
  315.3 142.5 all-reduce.9
where the time goes:
time: 556 us; the launch traced here: 550 us
  local copies, waits for them, and re-layouts  144 us (26%)
  waiting for transfers between devices  143 us (26%)
  other arithmetic  94 us (17%)
  blocking collectives  65.3 us (12%)
  matrix products  53.1 us (10%)
  starting transfers between devices  35.5 us (6%)
  between operations  15.1 us (3%)
    psum x1, waiting for transfers between devices, on_device(): lax.psum((totals[0], totals[1], totals[2], totals[3], totals[4], totals[5...  141 us
    psum x1, blocking collectives, on_device(): lax.psum((totals[0], totals[1], totals[2], totals[3], totals[4], totals[5...  65.3 us
    concatenate x4, other arithmetic, padded_2(): value = jnp.concatenate([before, value, after], axis=dim)  42.8 us
    slice x4, local copies, waits for them, and re-layouts, padded_2(): last = lax.slice_in_dim(value, length - width, length, axis=dim)  31.7 us
    dot_general x6, matrix products, vertical(): jnp.dot(weight_mid.T, first, precision=hp) + bias_mid[:, None]  23.4 us
    squeeze x2, local copies, waits for them, and re-layouts, on_device(): across = transport(padded[0], padded[1], padded[2], weighted)  20 us
    dot_general x6, matrix products, vertical(): jnp.dot(weight_in.T, columns, precision=hp) + bias_in[:, None]  18.3 us
    gather x1, local copies, waits for them, and re-layouts, on_device(): outgoing = stored[0][row_index]  17.1 us
  transfers between devices with their start and end apart: 10, of which 2 were waited for; matrix products, arithmetic and copies ran while one was open for 21% of the time, Pallas kernels for 0%

commit v1 on v0

--- a/solution.py
+++ b/solution.py
@@ -99,9 +99,9 @@
         down = grad_state.reshape(TRACERS, NZ, tile_x, tile_y)
         lam = lam + step_size * (across + down)
         totals = jax.tree.map(lambda left, right: left + step_size * right, totals, grad_params)
-    summed = lax.psum(
-        (totals[0], totals[1], totals[2], totals[3], totals[4], totals[5]), ("gx", "gy")
-    )
+    summed = (totals[0], totals[1], totals[2], totals[3], totals[4], totals[5])
+    for at in ("gx", "gy"):
+        summed = jax.lax.psum(summed, at)
     scale = 1.0 / jnp.sqrt(jnp.float32(ncols * devices))
     return (
         lam,

time: 556 us -> 516 us (0.928)
  waiting for transfers between devices: 143 us -> 67.6 us
  blocking collectives: 65.3 us -> 93.9 us
    psum x1 -> x2, waiting for transfers between devices: 141 us -> 65.6 us  [on_device(): summed = jax.lax.psum(summed, at)]
    psum x1 -> x2, blocking collectives: 65.3 us -> 93.9 us  [on_device(): summed = jax.lax.psum(summed, at)]
    unnamed x95 -> x99, local copies, waits for them, and re-layouts: 11.2 us -> 15 us
  transfers between devices with their start and end apart: 10 -> 11, of which waited for: 2 -> 3; matrix products, arithmetic and copies ran while one was open for 21% -> 35% of each run, Pallas kernels for 0% -> 0%
where the time goes in v1:
time: 516 us; the launch traced here: 508 us
  local copies, waits for them, and re-layouts  147 us (28%)
  other arithmetic  94.8 us (18%)
  blocking collectives  93.9 us (18%)
  waiting for transfers between devices  67.6 us (13%)
  matrix products  54.3 us (11%)
  starting transfers between devices  35.2 us (7%)
  between operations  15.1 us (3%)
    psum x2, blocking collectives, on_device(): summed = jax.lax.psum(summed, at)  93.9 us
    psum x2, waiting for transfers between devices, on_device(): summed = jax.lax.psum(summed, at)  65.6 us
    concatenate x4, other arithmetic, padded_2(): value = jnp.concatenate([before, value, after], axis=dim)  42.6 us
    slice x4, local copies, waits for them, and re-layouts, padded_2(): last = lax.slice_in_dim(value, length - width, length, axis=dim)  31.7 us
    dot_general x6, matrix products, vertical(): jnp.dot(weight_mid.T, first, precision=hp) + bias_mid[:, None]  23.4 us
    squeeze x2, local copies, waits for them, and re-layouts, on_device(): across = transport(padded[0], padded[1], padded[2], weighted)  20 us
    dot_general x6, matrix products, vertical(): jnp.dot(weight_in.T, columns, precision=hp) + bias_in[:, None]  19.5 us
    gather x1, local copies, waits for them, and re-layouts, on_device(): outgoing = stored[0][row_index]  17.1 us
  transfers between devices with their start and end apart: 11, of which 3 were waited for; matrix products, arithmetic and copies ran while one was open for 35% of the time, Pallas kernels for 0%

profile of v1, /device:TPU:32, one launch (start us, length us, event | category | flops | bytes accessed | tf_op | source)
XLA Modules:
  0.0 508.2 jit_solution(7650229565232812615)
XLA Ops:
  7.9 2.9 fusion.48
  17.0 3.4 copy.68
  21.0 17.1 %gather_fusion = bf16[4096,360]{1,0:T(8,128)(2,1)} fusion(bf16[4096,360]{1,0:T(8,128)(2,1)S(1)} %bitcast.88, s32[4096]{0:T(1024)S(1)} %broadcast_clamp_fusion), kind=kCustom, calls=%fused_computation | custom fusion | bytes 5914624 | tf_op jit(solution)/shard_map/gather | solution.py:83
  38.1 11.9 %all-to-all-start = ((bf16[128,32,360]{2,1,0:T(8,128)(2,1)}), bf16[128,32,360]{2,1,0:T(8,128)(2,1)S(1)}, u32[]{:S(2)}, u32[]{:S(2)}) async-start(bf16[128,32,360]{2,1,0:T(8,128)(2,1)} %bitcast.94), calls=%async_computation | async-start | bytes 6291456 | tf_op jit(solution)/shard_map/all_to_all | solution.py:84
  50.2 5.1 pad_maximum_fusion.2
  55.2 11.3 %fusion.61 = (f32[3,3,60,18,1]{4,3,2,1,0:T(8,128)}, f32[3,3,60,18,1]{4,3,2,1,0:T(8,128)}) fusion(f32[3,3,60,18,128]{4,3,2,1,0:T(8,128)} %pad_maximum_fusion.2), kind=kLoop, calls=%fused_computation.134 | loop fusion | bytes 155520 | tf_op jit(solution)/shard_map/slice | solution.py:20
  66.6 4.5 copy.64
  71.1 3.4 collective-permute-start.2
  74.5 5.2 %copy.65 = f32[3,3,60,18,1]{2,4,3,1,0:T(1,128)} copy(f32[3,3,60,18,1]{4,3,2,1,0:T(8,128)} %get-tuple-element.48) | data formatting | bytes 77760 | tf_op jit(solution)/shard_map/slice | solution.py:21
  79.7 4.8 collective-permute-start.3
  84.4 2.7 reshape_reshape.6
  89.2 5.2 %copy.66 = f32[3,3,60,18,1]{4,3,2,1,0:T(8,128)} copy(f32[3,3,60,18,1]{2,4,3,1,0:T(1,128)} %collective-permute-done.2) | data formatting | bytes 77760 | tf_op jit(solution)/shard_map/ppermute | solution.py:22
  94.3 5.2 %copy.67 = f32[3,3,60,18,1]{4,3,2,1,0:T(8,128)} copy(f32[3,3,60,18,1]{2,4,3,1,0:T(1,128)} %collective-permute-done.3) | data formatting | bytes 77760 | tf_op jit(solution)/shard_map/ppermute | solution.py:23
  99.6 16.7 %pad_maximum_fusion = f32[3,3,60,18,130]{4,3,2,1,0:T(8,128)} fusion(f32[3,3,60,18,1]{4,3,2,1,0:T(8,128)} %copy.67, f32[3,3,60,1,128]{4,3,2,1,0:T(1,128)} %collective-permute-done.1, f32[1,3,60,16,128]{4,3,2,1,0:T(8,128)} %copy-done.14, f32[1,3,60,16,128]{4,3,2,1,0:T(8,128)} %copy-done.13, f32[1,3,60,16,128]{4,3,2,1,0:T(8,128)} %copy-done.12, ...), kind=kLoop, calls=%fused_computation.2 | loop fusion | flops 7581600 | bytes 10108800 | tf_op jit(solution)/shard_map/concatenate | solution.py:24
  116.2 9.9 %slice_bitcast_fusion.5 = (f32[3,60,18,130]{3,2,1,0:T(8,128)}, f32[3,60,18,130]{3,2,1,0:T(8,128)}, f32[3,60,18,130]{3,2,1,0:T(8,128)}) fusion(f32[3,3,60,18,130]{4,3,2,1,0:T(8,128)} %pad_maximum_fusion), kind=kLoop, calls=%fused_computation.11 | loop fusion | bytes 10108800 | tf_op jit(solution)/shard_map/squeeze | solution.py:96
  126.1 9.3 %gather_fusion.1 = bf16[2048,360]{1,0:T(8,128)(2,1)} fusion(bf16[4096,360]{1,0:T(8,128)(2,1)S(1)} %bitcast.89, s32[2048]{0:T(1024)S(1)} %broadcast_clamp_fusion.1), kind=kCustom, calls=%fused_computation.1 | custom fusion | bytes 2957312 | tf_op jit(solution)/shard_map/gather | solution.py:85
  146.6 2.7 fusion.62
  149.3 3.3 copy.70
  152.6 2.8 reshape_reshape_squeeze.6
  155.4 2.9 fusion.59
  162.8 3.9 fusion.63
  168.2 4.5 fusion.4
  174.4 11.8 %fusion.49 = (f32[1,3,60,16,128]{4,3,2,1,0:T(8,128)}, f32[3,60,16,128]{3,2,1,0:T(8,128)S(1)}) fusion(f32[16,128]{1,0:T(8,128)S(1)} %convert_element_type.7, f32[3,60,16,128]{3,2,1,0:T(8,128)S(1)} %copy-done.33, f32[3,60,16,128]{3,2,1,0:T(8,128)S(1)} %bitcast.100, f32[3,60,18,130]{3,2,1,0:T(8,128)} %get-tuple-element.43, ...), kind=kLoop, calls=%fused_computation.106 | loop fusion | flops 6266880 | bytes 17702912 | tf_op jit(solution)/shard_map/stack | solution.py:94
  188.3 2.7 reshape_reshape.7
  191.0 3.5 fusion
  199.8 2.9 copy.75
  202.7 2.7 reshape_reshape_squeeze.7
  205.4 6.0 %fusion.58 = (f32[3,59,2048]{2,1,0:T(8,128)}, f32[3,59,2048]{2,1,0:T(8,128)}, f32[59,2048]{1,0:T(8,128)S(1)}) fusion(f32[3,60,2048]{2,1,0:T(8,128)} %reshape_reshape.7, f32[59,2048]{1,0:T(8,128)} %slice_multiply_fusion, f32[3,60,2048]{2,1,0:T(8,128)} %reshape_reshape_squeeze.7), kind=kLoop, calls=%fused_computation.131 | loop fusion | flops 2416640 | bytes 9666560 | tf_op jit(solution)/shard_map/transpose(jvp())/neg | solution.py:37
  215.9 4.3 fusion.67
  224.2 3.3 fusion.64
  227.5 25.9 %all-reduce.8 = (f32[256]{0:T(256)S(1)}, f32[256]{0:T(256)S(1)}, f32[256,60]{0,1:T(8,128)S(1)}, f32[60]{0:T(128)S(1)}) all-reduce(f32[256]{0:T(256)S(1)} %get-tuple-element.73, f32[256]{0:T(256)S(1)} %get-tuple-element.72, f32[256,60]{0,1:T(8,128)S(1)} %fusion.40, f32[60]{0:T(128)S(1)} %add_multiply_fusion.2), channel_id=1, replica_groups=mesh['gx'=8,'gy'=16] {'gx'}, use_global_device_ids=true, to_apply=%region_7.8 | all-reduce | flops 15932 | bytes 127456 | tf_op jit(solution)/shard_map/psum | solution.py:104
  253.4 68.0 %all-reduce.6 = (f32[256]{0:T(256)S(1)}, f32[256]{0:T(256)S(1)}, f32[256,60]{0,1:T(8,128)}, f32[60]{0:T(128)S(1)}) all-reduce(f32[256]{0:T(256)S(1)} %get-tuple-element.27, f32[256]{0:T(256)S(1)} %get-tuple-element.28, f32[256,60]{0,1:T(8,128)S(1)} %get-tuple-element.29, ...), channel_id=1, replica_groups=mesh['gx'=8,'gy'=16] {'gy'}, use_global_device_ids=true, to_apply=%region_8.9 | all-reduce | flops 15932 | bytes 127456 | tf_op jit(solution)/shard_map/psum | solution.py:104
  321.9 6.5 %fusion.38 = f32[256,256]{1,0:T(8,128)} fusion(f32[256,256]{1,0:T(8,128)} %fusion.67, f32[2048,256]{1,0:T(8,128)} %fusion.2, f32[2048,256]{1,0:T(8,128)} %copy-done.19), kind=kOutput, calls=%fused_computation.85 | convolution fusion | flops 1610743808 | bytes 4718592 | tf_op jit(solution)/shard_map/transpose(jvp())/dot_general | solution.py:32
  334.4 2.7 reshape.182
  337.1 3.7 fusion.39
  340.7 5.6 %fusion.5 = f32[180,2048]{1,0:T(8,128)} fusion(f32[180,2048]{1,0:T(8,128)} %reshape.182, f32[2048,256]{1,0:T(8,128)} %get-tuple-element.67, f32[180,256]{1,0:T(8,128)S(1)} %copy-done.35), kind=kOutput, calls=%fused_computation.27 | convolution fusion | flops 1132830720 | bytes 5230592 | tf_op jit(solution)/shard_map/transpose(jvp())/dot_general | solution.py:31
  347.6 4.6 pad_maximum_fusion.3
  352.2 11.3 %fusion.60 = (f32[3,3,60,18,1]{4,3,2,1,0:T(8,128)}, f32[3,3,60,18,1]{4,3,2,1,0:T(8,128)}) fusion(f32[3,3,60,18,128]{4,3,2,1,0:T(8,128)} %pad_maximum_fusion.3), kind=kLoop, calls=%fused_computation.133 | loop fusion | bytes 155520 | tf_op jit(solution)/shard_map/slice | solution.py:20
  363.5 4.5 copy.71
  370.0 4.8 copy.72
  374.8 6.0 %collective-permute-start.7 = (f32[3,3,60,18,1]{2,4,3,1,0:T(1,128)S(1)}, f32[3,3,60,18,1]{2,4,3,1,0:T(1,128)}, u32[]{:S(2)}, u32[]{:S(2)}) collective-permute-start(f32[3,3,60,18,1]{2,4,3,1,0:T(1,128)S(1)} %copy.72), channel_id=1, source_target_pairs={{1,0},{2,1},{3,2},{4,3},{5,4},{6,5},{7,6},{8,7},{9,8},{10,9},{11,1... | collective-permute-start | bytes 116648 | tf_op jit(solution)/shard_map/ppermute | solution.py:23
  384.3 26.3 %all-reduce.15.cloned.1.call-done = (f32[180,256]{1,0:T(8,128)}, f32[256,256]{1,0:T(8,128)}) async-done(((f32[180,256]{1,0:T(8,128)}, f32[256,256]{1,0:T(8,128)}), (f32[180,256]{1,0:T(8,128)}, f32[256,256]{1,0:T(8,128)})) %all-reduce.15.cloned.1.call-update) | async-done | bytes 446480 | tf_op jit(solution)/shard_map/psum | solution.py:104
  410.6 4.5 copy.73
  415.1 5.2 %copy.74 = f32[3,3,60,18,1]{4,3,2,1,0:T(8,128)} copy(f32[3,3,60,18,1]{2,4,3,1,0:T(1,128)} %collective-permute-done.7) | data formatting | bytes 77760 | tf_op jit(solution)/shard_map/ppermute | solution.py:23
  420.3 16.3 %pad_maximum_fusion.1 = f32[3,3,60,18,130]{4,3,2,1,0:T(8,128)} fusion(f32[3,3,60,18,1]{4,3,2,1,0:T(8,128)} %copy.74, f32[3,3,60,1,128]{4,3,2,1,0:T(1,128)} %collective-permute-done.5, f32[1,3,60,16,128]{4,3,2,1,0:T(8,128)S(1)} %copy-done.11, f32[1,3,60,16,128]{4,3,2,1,0:T(8,128)S(1)} %get-tuple-element.57, f32[1,3,60,16,128]{4,3,2,1,0:T(8,128)} %get-tuple-element.33, ...), kind=kLoop, calls=%fused_computation.3 | loop fusion | flops 7581600 | bytes 10108800 | tf_op jit(solution)/shard_map/concatenate | solution.py:24
  436.6 10.1 %slice_bitcast_fusion.2 = (f32[3,60,18,130]{3,2,1,0:T(8,128)}, f32[3,60,18,130]{3,2,1,0:T(8,128)}, f32[3,60,18,130]{3,2,1,0:T(8,128)}) fusion(f32[3,3,60,18,130]{4,3,2,1,0:T(8,128)} %pad_maximum_fusion.1), kind=kLoop, calls=%fused_computation.8 | loop fusion | bytes 10108800 | tf_op jit(solution)/shard_map/squeeze | solution.py:96
  446.6 11.7 %fusion.24 = f32[3,60,16,128]{3,2,1,0:T(8,128)} fusion(f32[3,60,16,128]{3,2,1,0:T(8,128)S(1)} %copy-done.22, f32[3,60,16,128]{3,2,1,0:T(8,128)S(1)} %bitcast.99, f32[3,60,18,130]{3,2,1,0:T(8,128)} %get-tuple-element.40, f32[3,60,18,130]{3,2,1,0:T(8,128)} %get-tuple-element.41, f32[3,60,18,130]{3,2,1,0:T(8,128)} %get-tuple-element.39, ...), kind=kLoop, calls=%fused_computation.57 | loop fusion | flops 5898240 | bytes 16228352 | tf_op jit(solution)/shard_map/add | solution.py:100
  458.3 39.3 %all-reduce.13.cloned.1.call-done = (f32[180,256]{1,0:T(8,128)}, f32[256,256]{1,0:T(8,128)}) async-done(((f32[180,256]{1,0:T(8,128)}, f32[256,256]{1,0:T(8,128)}), (f32[180,256]{1,0:T(8,128)}, f32[256,256]{1,0:T(8,128)})) %all-reduce.13.cloned.1.call-update) | async-done | bytes 446480 | tf_op jit(solution)/shard_map/psum | solution.py:104
  (155 shorter events, 60.3 us)
Async XLA Ops:
  7.2 133.6 %copy-start = (f32[256,256]{1,0:T(8,128)S(1)}, f32[256,256]{1,0:T(8,128)}, u32[]{:S(2)}) copy-start(f32[256,256]{1,0:T(8,128)} %param.22) | copy-start | bytes 786436
  10.8 2.3 copy-start.14
  13.1 37.0 %collective-permute-start = (f32[3,3,60,1,128]{4,3,2,1,0:T(1,128)}, f32[3,3,60,1,128]{4,3,2,1,0:T(1,128)}, u32[]{:S(2)}, u32[]{:S(2)}) collective-permute-start(f32[3,3,60,1,128]{4,3,2,1,0:T(1,128)} %get-tuple-element.51), channel_id=1, source_target_pairs={{0,16},{16,32},{32,48},{48,64},{64,80},{80,96},{96,112},{1,17},{17... | collective-permute-start | bytes 829448 | tf_op jit(solution)/shard_map/ppermute | solution.py:22
  15.5 4.8 copy-start.46
  15.5 34.6 %collective-permute-start.1 = (f32[3,3,60,1,128]{4,3,2,1,0:T(1,128)}, f32[3,3,60,1,128]{4,3,2,1,0:T(1,128)}, u32[]{:S(2)}, u32[]{:S(2)}) collective-permute-start(f32[3,3,60,1,128]{4,3,2,1,0:T(1,128)} %get-tuple-element.52), channel_id=1, source_target_pairs={{16,0},{32,16},{48,32},{64,48},{80,64},{96,80},{112,96},{17,1},{33... | collective-permute-start | bytes 829448 | tf_op jit(solution)/shard_map/ppermute | solution.py:23
  38.1 12.0 %copy-start.40 = (s32[16,128]{1,0:T(8,128)S(1)}, s32[16,128]{1,0:T(8,128)}, u32[]{:S(2)}) copy-start(s32[16,128]{1,0:T(8,128)} %param.15) | copy-start | bytes 24580
  38.1 88.0 %all-to-all-start = ((bf16[128,32,360]{2,1,0:T(8,128)(2,1)}), bf16[128,32,360]{2,1,0:T(8,128)(2,1)S(1)}, u32[]{:S(2)}, u32[]{:S(2)}) async-start(bf16[128,32,360]{2,1,0:T(8,128)(2,1)} %bitcast.94), calls=%async_computation | async-start | bytes 6291456 | tf_op jit(solution)/shard_map/all_to_all | solution.py:84
  50.1 360.5 %all-reduce.15.cloned.1.call-start = ((), (), s32[]{:S(2)}) async-start(), calls=%async_computation.2 | async-start | bytes 901120 | tf_op jit(solution)/shard_map/psum | solution.py:104
  71.1 18.1 %collective-permute-start.2 = (f32[3,3,60,18,1]{2,4,3,1,0:T(1,128)S(1)}, f32[3,3,60,18,1]{2,4,3,1,0:T(1,128)}, u32[]{:S(2)}, u32[]{:S(2)}) collective-permute-start(f32[3,3,60,18,1]{2,4,3,1,0:T(1,128)S(1)} %copy.64), channel_id=1, source_target_pairs={{0,1},{1,2},{2,3},{3,4},{4,5},{5,6},{6,7},{7,8},{8,9},{9,10},{10,1... | collective-permute-start | bytes 116648 | tf_op jit(solution)/shard_map/ppermute | solution.py:22
  79.7 14.7 %collective-permute-start.3 = (f32[3,3,60,18,1]{2,4,3,1,0:T(1,128)}, f32[3,3,60,18,1]{2,4,3,1,0:T(1,128)}, u32[]{:S(2)}, u32[]{:S(2)}) collective-permute-start(f32[3,3,60,18,1]{2,4,3,1,0:T(1,128)} %copy.65), channel_id=1, source_target_pairs={{1,0},{2,1},{3,2},{4,3},{5,4},{6,5},{7,6},{8,7},{9,8},{10,9},{11,1... | collective-permute-start | bytes 116648 | tf_op jit(solution)/shard_map/ppermute | solution.py:23
  138.4 4.3 copy-start.3
  138.4 2.4 copy-start.42
  140.8 1.9 copy-start.36
  140.8 1.9 copy-start.44
  142.7 2.2 copy-start.8
  152.6 2.8 copy-start.20
  155.4 2.9 copy-start.9
  155.4 2.9 copy-start.24
  158.3 2.1 copy-start.28
  160.4 6.3 %copy-start.16 = (f32[2048,256]{1,0:T(8,128)}, f32[2048,256]{1,0:T(8,128)S(1)}, u32[]{:S(2)}) copy-start(f32[2048,256]{1,0:T(8,128)S(1)} %get-tuple-element.69) | copy-start | bytes 6291460
  160.5 2.3 copy-start.4
  174.4 11.8 %copy-start.38 = (f32[16,128]{1,0:T(8,128)S(1)}, f32[16,128]{1,0:T(8,128)}, u32[]{:S(2)}) copy-start(f32[16,128]{1,0:T(8,128)} %param.17) | copy-start | bytes 24580
  174.4 11.8 %copy-start.39 = (f32[16,128]{1,0:T(8,128)S(1)}, f32[16,128]{1,0:T(8,128)}, u32[]{:S(2)}) copy-start(f32[16,128]{1,0:T(8,128)} %param.18) | copy-start | bytes 24580
  186.1 2.1 copy-start.21
  191.0 4.9 copy-start.45
  205.4 6.0 %copy-start.7 = (f32[2048,256]{1,0:T(8,128)S(1)}, f32[2048,256]{1,0:T(8,128)}, u32[]{:S(2)}) copy-start(f32[2048,256]{1,0:T(8,128)} %copy-done.6) | copy-start | bytes 6291460
  205.4 6.0 %copy-start.27 = (f32[60,2048]{1,0:T(8,128)S(1)}, f32[60,2048]{1,0:T(8,128)}, u32[]{:S(2)}) copy-start(f32[60,2048]{1,0:T(8,128)} %copy-done.26) | copy-start | bytes 1474564
  211.4 2.3 copy-start.25
  211.4 2.3 copy-start.29
  211.4 2.5 copy-start.17
  213.5 10.5 %copy-start.19 = (f32[2048,256]{1,0:T(8,128)}, f32[2048,256]{1,0:T(8,128)S(1)}, u32[]{:S(2)}) copy-start(f32[2048,256]{1,0:T(8,128)S(1)} %get-tuple-element.71) | copy-start | bytes 6291460
  213.5 2.3 copy-start.5
  215.9 4.3 copy-start.18
  224.2 3.3 copy-start.43
  321.9 6.5 %copy-start.10 = (f32[1,3,60,16,128]{4,3,2,1,0:T(8,128)S(1)}, f32[1,3,60,16,128]{4,3,2,1,0:T(8,128)}, u32[]{:S(2)}) copy-start(f32[1,3,60,16,128]{4,3,2,1,0:T(8,128)} %get-tuple-element.58) | copy-start | bytes 4423684
  321.9 6.5 %copy-start.15 = (f32[1,3,60,16,128]{4,3,2,1,0:T(8,128)S(1)}, f32[1,3,60,16,128]{4,3,2,1,0:T(8,128)}, u32[]{:S(2)}) copy-start(f32[1,3,60,16,128]{4,3,2,1,0:T(8,128)} %get-tuple-element.33) | copy-start | bytes 4423684
  328.5 4.5 copy-start.30
  328.5 4.5 copy-start.31
  329.7 17.9 %collective-permute-start.4 = (f32[3,3,60,1,128]{4,3,2,1,0:T(1,128)}, f32[3,3,60,1,128]{4,3,2,1,0:T(1,128)}, u32[]{:S(2)}, u32[]{:S(2)}) collective-permute-start(f32[3,3,60,1,128]{4,3,2,1,0:T(1,128)} %get-tuple-element.49), channel_id=1, source_target_pairs={{0,16},{16,32},{32,48},{48,64},{64,80},{80,96},{96,112},{1,17},{17... | collective-permute-start | bytes 829448 | tf_op jit(solution)/shard_map/ppermute | solution.py:22
  331.7 15.9 %collective-permute-start.5 = (f32[3,3,60,1,128]{4,3,2,1,0:T(1,128)}, f32[3,3,60,1,128]{4,3,2,1,0:T(1,128)}, u32[]{:S(2)}, u32[]{:S(2)}) collective-permute-start(f32[3,3,60,1,128]{4,3,2,1,0:T(1,128)} %get-tuple-element.50), channel_id=1, source_target_pairs={{16,0},{32,16},{48,32},{64,48},{80,64},{96,80},{112,96},{17,1},{33... | collective-permute-start | bytes 829448 | tf_op jit(solution)/shard_map/ppermute | solution.py:23
  337.1 3.7 copy-start.35
  340.7 6.2 %copy-start.37 = (f32[256,60]{0,1:T(8,128)S(1)}, f32[256,60]{0,1:T(8,128)}, u32[]{:S(2)}) copy-start(f32[256,60]{0,1:T(8,128)} %get-tuple-element.23) | copy-start | bytes 184324
  340.7 6.9 %copy-start.11 = (f32[1,3,60,16,128]{4,3,2,1,0:T(8,128)S(1)}, f32[1,3,60,16,128]{4,3,2,1,0:T(8,128)}, u32[]{:S(2)}) copy-start(f32[1,3,60,16,128]{4,3,2,1,0:T(8,128)} %get-tuple-element.58) | copy-start | bytes 4423684
  346.9 150.7 %all-reduce.13.cloned.1.call-start = ((), (), s32[]{:S(2)}) async-start(), calls=%async_computation.1 | async-start | bytes 901120 | tf_op jit(solution)/shard_map/psum | solution.py:104
  368.0 42.5 %collective-permute-start.6 = (f32[3,3,60,18,1]{2,4,3,1,0:T(1,128)S(1)}, f32[3,3,60,18,1]{2,4,3,1,0:T(1,128)S(1)}, u32[]{:S(2)}, u32[]{:S(2)}) collective-permute-start(f32[3,3,60,18,1]{2,4,3,1,0:T(1,128)S(1)} %copy.71), channel_id=1, source_target_pairs={{0,1},{1,2},{2,3},{3,4},{4,5},{5,6},{6,7},{7,8},{8,9},{9,10},{10,1... | collective-permute-start | bytes 116648 | tf_op jit(solution)/shard_map/ppermute | solution.py:22
  374.8 40.3 %collective-permute-start.7 = (f32[3,3,60,18,1]{2,4,3,1,0:T(1,128)S(1)}, f32[3,3,60,18,1]{2,4,3,1,0:T(1,128)}, u32[]{:S(2)}, u32[]{:S(2)}) collective-permute-start(f32[3,3,60,18,1]{2,4,3,1,0:T(1,128)S(1)} %copy.72), channel_id=1, source_target_pairs={{1,0},{2,1},{3,2},{4,3},{5,4},{6,5},{7,6},{8,7},{9,8},{10,9},{11,1... | collective-permute-start | bytes 116648 | tf_op jit(solution)/shard_map/ppermute | solution.py:23
  436.5 10.1 %copy-start.22 = (f32[3,60,16,128]{3,2,1,0:T(8,128)S(1)}, f32[3,60,16,128]{3,2,1,0:T(8,128)}, u32[]{:S(2)}) copy-start(f32[3,60,16,128]{3,2,1,0:T(8,128)} %copy-done.21) | copy-start | bytes 4423684
  436.6 10.1 %copy-start.32 = (f32[180,16,128]{2,1,0:T(8,128)S(1)}, f32[180,16,128]{2,1,0:T(8,128)}, u32[]{:S(2)}) copy-start(f32[180,16,128]{2,1,0:T(8,128)} %slice.203) | copy-start | bytes 4423684
  (10 other events, 14.9 us)
Sparse Core Ops, SparseCore 0:
  347.0 63.5 all-reduce.14
  414.3 83.2 all-reduce.12
